TPU v7x, 256 devices: a whole 4x4x8 slice. The times are simulated.
256 devices in a mesh: dp: 4 (over x), expert: 32 (over z, y), tensor: 2 (over core).
Axes of the slice: x: 4, y: 4, z: 8, core: 2. Of those that a mesh axis runs over, the one named last changes fastest.
Arguments:
- queries: bfloat16 [8192, 4096], P(('dp', 'expert'), 'tensor'), may hold values from -8 to 8
- fresh_keys: bfloat16 [8192, 512], P(('dp', 'expert'), 'tensor'), may hold values from -6 to 6
- fresh_values: bfloat16 [8192, 512], P(('dp', 'expert'), 'tensor'), may hold values from -6 to 6
- resident_keys: bfloat16 [128, 2048, 512], P(('dp', 'expert'), None, 'tensor'), may hold values from -8 to 8
- resident_values: bfloat16 [128, 2048, 512], P(('dp', 'expert'), None, 'tensor'), may hold values from -6 to 6
- out_weight: bfloat16 [4096, 2048], P('tensor', 'dp'), may hold values from -0.5 to 0.5
- residual: bfloat16 [8192, 2048], P(('dp', 'expert')), may hold values from -23 to 23
- norm_gain: float32 [2048], replicated, may hold values from 0.1 to 1.9
- expert_ids: int32 [8192, 8], P(('dp', 'expert')), may hold values from 0 to 127, all different within a row; in each aligned block of 64 rows (0 to 63, 64 to 127, ...) at most 6 rows name the same one
- gates: float32 [8192, 8], P(('dp', 'expert')), may hold values from 0.05 to 0.5
- w_gate: bfloat16 [128, 2048, 768], P(('dp', 'expert'), None, 'tensor'), may hold values from -0.125 to 0.125
- w_up: bfloat16 [128, 2048, 768], P(('dp', 'expert'), None, 'tensor'), may hold values from -0.125 to 0.125
- w_down: bfloat16 [128, 768, 2048], P(('dp', 'expert'), 'tensor'), may hold values from -0.21875 to 0.21875
Outputs:
- mixed: bfloat16 [8192, 2048], P(('dp', 'expert'), 'tensor')
Inputs may be any that keep to these rules, and one draw needn't show every extreme that they name: `expert_ids`: within the 64 tokens of one sequence no expert is named by more than 6 tokens, a bound that some block reaches; a token names 8 different experts.
All inputs are finite; a program needn't handle non-finite values.
Results may differ from a plain program's by a relative error of at most 0.0085.
Values may be sent and summed in bfloat16 or wider, within the bound.
No kernel may reach another device: no remote copies, remote signals or barrier semaphores. Data moves between devices by JAX's collectives and lax.ppermute only.
A program may use at most 64 MiB of HBM per device.

v0:
```python
import jax
import jax.numpy as jnp
from jax import lax
from jax.sharding import PartitionSpec as P

D = 2048
HEAD_WIDTH = 128


def attend_local(queries, fresh_keys, fresh_values, resident_keys, resident_values):
    tokens_here = queries.shape[0]
    kv_here = fresh_keys.shape[1] // HEAD_WIDTH
    query_group = queries.shape[1] // HEAD_WIDTH // kv_here
    context = resident_keys.shape[1]
    query_rows = queries.reshape(tokens_here, kv_here, query_group, HEAD_WIDTH)
    joined_keys = jnp.concatenate([resident_keys[0], fresh_keys], 0).reshape(
        context + tokens_here, kv_here, HEAD_WIDTH
    )
    joined_values = jnp.concatenate([resident_values[0], fresh_values], 0).reshape(
        context + tokens_here, kv_here, HEAD_WIDTH
    )
    score = jnp.einsum(
        "tjgd,sjd->jgts", query_rows, joined_keys, preferred_element_type=jnp.float32
    ) * HEAD_WIDTH ** (-0.5)
    places = jnp.arange(context + tokens_here)
    rows = jnp.arange(tokens_here)
    allowed = (places[None, :] < context) | (places[None, :] - context <= rows[:, None])
    score = jnp.where(allowed, score, jnp.float32(-1e30))
    top_score = jnp.max(score, axis=-1, keepdims=True)
    weight = jnp.exp(score - top_score)
    probs = (weight / jnp.sum(weight, axis=-1, keepdims=True)).astype(jnp.bfloat16)
    attended = jnp.einsum(
        "jgts,sjd->tjgd", probs, joined_values, preferred_element_type=jnp.float32
    )
    return attended.reshape(tokens_here, -1).astype(jnp.bfloat16)


def expert_rows(block, gate_mat, up_mat, down_mat):
    sources, items, width = block.shape
    flat = block.reshape(sources * items, width)
    gate_part = jnp.dot(flat, gate_mat, preferred_element_type=jnp.float32)
    up_part = jnp.dot(flat, up_mat, preferred_element_type=jnp.float32)
    act = (jax.nn.silu(gate_part) * up_part).astype(jnp.bfloat16)
    result = jnp.dot(act, down_mat, preferred_element_type=jnp.float32)
    return result.reshape(sources, items, -1)


def per_device(
    queries,
    fresh_keys,
    fresh_values,
    resident_keys,
    resident_values,
    out_weight,
    residual,
    norm_gain,
    expert_ids,
    gates,
    w_gate,
    w_up,
    w_down,
):
    attended = attend_local(queries, fresh_keys, fresh_values, resident_keys, resident_values)
    partial_sum = jnp.dot(
        attended,
        lax.all_gather(out_weight, "dp", axis=1, tiled=True),
        preferred_element_type=jnp.float32,
    )
    tokens_here = residual.shape[0]
    pairs = lax.axis_size("tensor")
    half = D // pairs
    lane = lax.axis_index("tensor")
    summed = lax.psum(partial_sum.astype(jnp.bfloat16), "tensor").astype(jnp.float32)
    hidden = residual.astype(jnp.float32) + summed
    mean_square = jnp.mean(hidden * hidden, axis=-1, keepdims=True)
    normed = (hidden * lax.rsqrt(mean_square + 1e-06) * norm_gain).astype(jnp.bfloat16)
    hidden_half = lax.dynamic_slice_in_dim(hidden, lane * half, half, 1)
    owners = lax.axis_size("dp") * lax.axis_size("expert")
    top = expert_ids.shape[1]
    slots = max(2, tokens_here * top * 3 // (2 * owners))
    onehot = (expert_ids[:, :, None] == jnp.arange(owners)[None, None, :]).astype(jnp.int32)
    per_token = jnp.sum(onehot, axis=1)
    before = jnp.cumsum(per_token, axis=0) - per_token
    slot = jnp.sum(onehot * before[:, None, :], axis=-1)
    token_rows = jnp.broadcast_to(
        jnp.arange(tokens_here, dtype=jnp.int32)[:, None], expert_ids.shape
    )
    owner_rows = jnp.full((owners, slots), -1, jnp.int32).at[expert_ids, slot].set(token_rows)
    valid = owner_rows >= 0
    outgoing = jnp.where(
        valid[:, :, None], normed[jnp.maximum(owner_rows, 0)], jnp.zeros((), jnp.bfloat16)
    )
    expert_part = expert_rows(
        lax.all_to_all(outgoing, ("dp", "expert"), split_axis=0, concat_axis=0, tiled=True),
        w_gate[0],
        w_up[0],
        w_down[0],
    )
    owned = lax.psum_scatter(
        expert_part.astype(jnp.bfloat16), "tensor", scatter_dimension=2, tiled=True
    )
    returned = lax.all_to_all(owned, ("dp", "expert"), split_axis=0, concat_axis=0, tiled=True)
    picked = returned[expert_ids, slot]
    moe = jnp.sum(gates[:, :, None] * picked.astype(jnp.float32), axis=1)
    return (hidden_half + moe).astype(jnp.bfloat16)


def solution(mesh):
    return jax.shard_map(
        per_device,
        mesh=mesh,
        in_specs=(
            P(("dp", "expert"), "tensor"),
            P(("dp", "expert"), "tensor"),
            P(("dp", "expert"), "tensor"),
            P(("dp", "expert"), None, "tensor"),
            P(("dp", "expert"), None, "tensor"),
            P("tensor", "dp"),
            P(("dp", "expert"), None),
            P(),
            P(("dp", "expert"), None),
            P(("dp", "expert"), None),
            P(("dp", "expert"), None, "tensor"),
            P(("dp", "expert"), None, "tensor"),
            P(("dp", "expert"), "tensor", None),
        ),
        out_specs=P(("dp", "expert"), "tensor"),
        check_vma=False,
    )
```

profile of v0, /device:TPU:32, one launch (start us, length us, event | category | flops | bytes accessed | tf_op | source)
XLA Modules:
  0.0 379.2 jit_solution(17011101792321861209)
XLA Ops:
  6.5 0.0 copy-start
  6.5 0.0 all-gather.2.cloned.1.call-start
  6.5 0.7 all-gather.2.cloned.1.call-update
  7.3 0.0 copy-start.4
  7.3 0.0 all-reduce.2.cloned.1.call-start
  7.3 1.5 copy.74
  8.8 1.4 copy.75
  10.2 0.0 copy-done.4
  10.3 0.0 copy-start.5
  10.3 0.0 copy-start.6
  10.3 1.5 copy.71
  11.8 1.3 copy.72
  13.1 0.0 copy-done.5
  13.1 0.0 copy-done.6
  13.1 0.1 fusion.26
  13.3 0.0 copy-start.2
  13.3 4.6 %fusion.46 = f32[2,8,64]{2,1,0:T(8,128)S(1)} fusion(pred[64,2112]{1,0:T(8,128)(4,1)S(1)} %fusion.26, bf16[64,2,128]{2,0,1:T(8,128)(2,1)S(1)} %get-tuple-element.9, bf16[2048,2,128]{2,0,1:T(8,128)(2,1)} %copy.75, bf16[64,2,8,128]{3,2,1,0:T(8,128)(2,1)S(1)} %bitcast.97), kind=kOutput, calls=%fused_computation.69 | convolution fusion | flops 564463680 | bytes 1482752 | tf_op jit(solution)/shard_map/sub | solution.py:30
  17.9 0.0 copy-done.2
  17.9 4.9 %fusion.19 = bf16[64,2,8,128]{3,0,2,1:T(8,128)(2,1)S(1)} fusion(f32[2,8,64]{2,1,0:T(8,128)S(1)} %fusion.46, bf16[64,2,128]{2,0,1:T(8,128)(2,1)S(1)} %get-tuple-element.10, bf16[2048,2,128]{2,0,1:T(8,128)(2,1)} %copy.72, pred[64,2112]{1,0:T(8,128)(4,1)S(1)} %fusion.26, bf16[64,2,128]{2,0,1:T(8,128)(2,1)S(1)} %get-tuple-element.9, ...), kind=kOutput, calls=%fused_computation.25 | convolution fusion | flops 1122569216 | bytes 2826240 | tf_op jit(solution)/shard_map/jgts,sjd->tjgd/dot_general | solution.py:32
  22.8 0.2 copy.78
  23.0 0.0 copy-done.7
  23.0 0.1 copy.80
  23.1 0.1 convert_reduce_fusion
  23.3 0.1 reduce_window_sum.11
  23.4 1.2 select_reduce_fusion
  24.6 0.1 copy.81
  24.7 0.1 copy.82
  24.8 0.1 reshape.80
  24.9 0.1 reshape.82
  25.0 22.0 %scatter_fusion = s32[128,6]{0,1:T(8,128)S(1)} fusion(s32[128,6]{0,1:T(8,128)S(1)} %broadcast_in_dim.26, s32[512]{0:T(512)S(1)} %reshape.80, s32[512]{0:T(512)S(1)} %reshape.82), kind=kCustom, calls=%fused_computation.2 | custom fusion | bytes 10240 | tf_op jit(solution)/shard_map/scatter | solution.py:88
  47.0 0.1 copy.84
  47.1 0.1 reshape.68
  47.3 50.1 %all-gather.2.cloned.1.call-done = bf16[2048,2048]{1,0:T(8,128)(2,1)} async-done(((bf16[2048,512]{1,0:T(8,128)(2,1)}), bf16[2048,2048]{1,0:T(8,128)(2,1)}) %all-gather.2.cloned.1.call-update) | async-done | bytes 8388624 | tf_op jit(solution)/shard_map/all_gather | solution.py:66
  97.4 5.7 %convolution_convert_fusion.1 = bf16[64,2048]{1,0:T(8,128)(2,1)} fusion(bf16[2048,2048]{1,0:T(8,128)(2,1)} %all-gather.2.cloned.1.call-done, bf16[8,8,16,128]{3,2,1,0:T(8,128)(2,1)S(1)} %bitcast.95), kind=kOutput, calls=%fused_computation.14 | convolution fusion | flops 537001984 | bytes 8912896 | tf_op jit(solution)/shard_map/dot_general | solution.py:64
  103.1 0.0 all-reduce.2.cloned.1.call-update
  103.1 0.2 reduce-scatter.2.cloned.1.call-start
  103.4 0.1 copy.83
  103.5 29.8 %all-reduce.2.cloned.1.call-done = bf16[64,2048]{1,0:T(8,128)(2,1)} async-done(((bf16[64,2048]{1,0:T(8,128)(2,1)}), bf16[64,2048]{1,0:T(8,128)(2,1)}) %all-reduce.2.cloned.1.call-update) | async-done | bytes 262160 | tf_op jit(solution)/shard_map/psum | solution.py:73
  133.3 0.0 copy-done.3
  133.3 1.9 convert_add_fusion
  135.3 1.1 multiply_convert_fusion
  136.3 4.3 %gather_fusion = bf16[768,2048]{1,0:T(8,128)(2,1)} fusion(bf16[64,2048]{1,0:T(8,128)(2,1)S(1)} %multiply_convert_fusion, s32[1024]{0:T(1024)S(1)} %pad_clamp_fusion), kind=kCustom, calls=%fused_computation | custom fusion | bytes 6294528 | tf_op jit(solution)/shard_map/gather | solution.py:91
  140.6 6.3 %reshape.67 = bf16[128,6,2048]{2,1,0:T(8,128)(2,1)} reshape(bf16[768,2048]{1,0:T(8,128)(2,1)} %gather_fusion) | data formatting | bytes 6291456 | tf_op jit(solution)/shard_map/gather | solution.py:91
  146.9 2.6 broadcast_select_fusion
  149.5 111.2 %all_to_all.10 = bf16[128,6,2048]{2,1,0:T(8,128)(2,1)} all-to-all(bf16[128,6,2048]{2,1,0:T(8,128)(2,1)S(1)} %broadcast_select_fusion), channel_id=1, replica_groups=mesh['dp'=4,'expert'=32,'tensor'=2] {'dp','expert'}, dimensions={0} | all-to-all | bytes 6291456 | tf_op jit(solution)/shard_map/all_to_all | solution.py:94
  260.8 6.3 %reshape.65 = bf16[768,2048]{1,0:T(8,128)(2,1)} reshape(bf16[128,6,2048]{2,1,0:T(8,128)(2,1)} %all_to_all.10) | data formatting | bytes 6291456 | tf_op jit(solution)/shard_map/reshape | solution.py:40
  267.1 4.3 %fusion.10 = f32[768,384]{1,0:T(8,128)S(1)} fusion(bf16[768,2048]{1,0:T(8,128)(2,1)} %reshape.65, bf16[1,2048,384]{2,1,0:T(8,128)(2,1)} %param.23), kind=kOutput, calls=%fused_computation.20 | convolution fusion | flops 1207959552 | bytes 5898240 | tf_op jit(solution)/shard_map/dot_general | solution.py:41
  271.4 0.0 copy-done.1
  271.4 0.0 copy-done.10
  271.4 1.8 fusion.15
  273.3 0.2 dot_general.25
  273.5 3.5 convolution_convert_fusion
  276.9 0.0 reduce-scatter.2.cloned.1.call-update
  277.0 11.5 %reduce-scatter.2.cloned.1.call-done = bf16[128,6,1024]{2,0,1:T(8,128)(2,1)} async-done(((bf16[128,6,2048]{2,0,1:T(8,128)(2,1)}), bf16[128,6,1024]{2,0,1:T(8,128)(2,1)}) %reduce-scatter.2.cloned.1.call-update) | async-done | bytes 1572880 | tf_op jit(solution)/shard_map/reduce_scatter | solution.py:99
  288.4 3.6 copy.86
  292.1 14.3 %all-to-all-start.1 = ((bf16[128,6,1024]{2,1,0:T(8,128)(2,1)}), bf16[128,6,1024]{2,1,0:T(8,128)(2,1)}, u32[]{:S(2)}, u32[]{:S(2)}) async-start(bf16[128,6,1024]{2,1,0:T(8,128)(2,1)} %copy.86), calls=%async_computation.2 | async-start | bytes 4194304 | tf_op jit(solution)/shard_map/all_to_all | solution.py:102
  306.4 0.1 copy.87
  306.5 0.1 reshape.74
  306.6 0.1 copy.79
  306.7 52.1 %all-to-all-done.1 = bf16[128,6,1024]{2,1,0:T(8,128)(2,1)} async-done(((bf16[128,6,1024]{2,1,0:T(8,128)(2,1)}), bf16[128,6,1024]{2,1,0:T(8,128)(2,1)}, u32[]{:S(2)}, u32[]{:S(2)}) %all-to-all-start.1) | async-done | bytes 1572896 | tf_op jit(solution)/shard_map/all_to_all | solution.py:102
  358.8 2.5 copy.88
  361.2 7.9 %gather_fusion.1 = bf16[512,1024]{1,0:T(8,128)(2,1)} fusion(bf16[128,6,1024]{2,0,1:T(8,128)(2,1)S(1)} %copy.88, s32[512]{0:T(512)S(1)} %reshape.74), kind=kCustom, calls=%fused_computation.1 | custom fusion | bytes 2101248 | tf_op jit(solution)/shard_map/gather | solution.py:103
  369.1 1.9 fusion.6
  371.0 1.6 add_convert_fusion
  (21 shorter events, 0.1 us)
Async XLA Ops:
  6.5 266.9 %copy-start = (bf16[1,384,2048]{2,1,0:T(8,128)(2,1)S(1)}, bf16[1,384,2048]{2,1,0:T(8,128)(2,1)}, u32[]{:S(2)}) copy-start(bf16[1,384,2048]{2,1,0:T(8,128)(2,1)} %param.25) | copy-start | bytes 4718596
  6.5 90.8 %all-gather.2.cloned.1.call-start = ((), (), s32[]{:S(2)}) async-start(), calls=%async_computation.3 | async-start | bytes 10485760 | tf_op jit(solution)/shard_map/all_gather | solution.py:66
  7.3 3.0 copy-start.4
  7.3 126.1 %all-reduce.2.cloned.1.call-start = ((), (), s32[]{:S(2)}) async-start(), calls=%async_computation.4 | async-start | bytes 524288 | tf_op jit(solution)/shard_map/psum | solution.py:73
  10.3 2.8 copy-start.5
  10.3 2.8 copy-start.6
  13.3 4.7 %copy-start.2 = (bf16[2048,2,128]{2,0,1:T(8,128)(2,1)S(1)}, bf16[2048,2,128]{2,0,1:T(8,128)(2,1)}, u32[]{:S(2)}) copy-start(bf16[2048,2,128]{2,0,1:T(8,128)(2,1)} %copy.75) | copy-start | bytes 3145732
  17.9 5.1 %copy-start.7 = (s32[64,8]{0,1:T(8,128)S(1)}, s32[64,8]{0,1:T(8,128)}, u32[]{:S(2)}) copy-start(s32[64,8]{0,1:T(8,128)} %param.21) | copy-start | bytes 6148
  97.4 35.9 %copy-start.3 = (bf16[64,2048]{1,0:T(8,128)(2,1)S(1)}, bf16[64,2048]{1,0:T(8,128)(2,1)}, u32[]{:S(2)}) copy-start(bf16[64,2048]{1,0:T(8,128)(2,1)} %param.19) | copy-start | bytes 786436
  97.4 37.9 %copy-start.8 = (f32[2048]{0:T(1024)S(1)}, f32[2048]{0:T(1024)}, u32[]{:S(2)}) copy-start(f32[2048]{0:T(1024)} %param.20) | copy-start | bytes 24580
  103.1 185.3 %reduce-scatter.2.cloned.1.call-start = ((), (), s32[]{:S(2)}) async-start(), calls=%async_computation.5 | async-start | bytes 4718592 | tf_op jit(solution)/shard_map/reduce_scatter | solution.py:99
  267.1 4.3 %copy-start.1 = (bf16[768,2048]{1,0:T(8,128)(2,1)S(1)}, bf16[768,2048]{1,0:T(8,128)(2,1)}, u32[]{:S(2)}) copy-start(bf16[768,2048]{1,0:T(8,128)(2,1)} %reshape.65) | copy-start | bytes 9437188
  267.1 4.3 %copy-start.10 = (bf16[1,2048,384]{2,1,0:T(8,128)(2,1)S(1)}, bf16[1,2048,384]{2,1,0:T(8,128)(2,1)}, u32[]{:S(2)}) copy-start(bf16[1,2048,384]{2,1,0:T(8,128)(2,1)} %param.24) | copy-start | bytes 4718596
  292.1 14.5 %copy-start.9 = (f32[64,8]{0,1:T(8,128)S(1)}, f32[64,8]{0,1:T(8,128)}, u32[]{:S(2)}) copy-start(f32[64,8]{0,1:T(8,128)} %param.22) | copy-start | bytes 6148
  292.1 66.7 %all-to-all-start.1 = ((bf16[128,6,1024]{2,1,0:T(8,128)(2,1)}), bf16[128,6,1024]{2,1,0:T(8,128)(2,1)}, u32[]{:S(2)}, u32[]{:S(2)}) async-start(bf16[128,6,1024]{2,1,0:T(8,128)(2,1)} %copy.86), calls=%async_computation.2 | async-start | bytes 4194304 | tf_op jit(solution)/shard_map/all_to_all | solution.py:102
Sparse Core Ops, SparseCore 0:
  9.1 88.1 all-gather.1
  103.2 30.0 all-reduce.1
  277.1 11.3 reduce-scatter.1
where the time goes:
time: 380 us; the launch traced here: 379 us
  waiting for transfers between devices  144 us (38%)
  blocking collectives  111 us (29%)
  local copies, waits for them, and re-layouts  60 us (16%)
  matrix products  24.9 us (7%)
  starting transfers between devices  14.6 us (4%)
  between operations  13.4 us (4%)
  other arithmetic  10.8 us (3%)
    all_to_all x1, blocking collectives, per_device(): lax.all_to_all(outgoing, ('dp', 'expert'), split_axis=0, concat_axis=0, t...  111 us
    all_to_all x1, waiting for transfers between devices, per_device(): lax.all_to_all(owned, ('dp', 'expert'), split_axis=0, concat_axis=0, tile...  52.1 us
    all_gather x1, waiting for transfers between devices, per_device(): lax.all_gather(out_weight, 'dp', axis=1, tiled=True)  50.1 us
    psum x1, waiting for transfers between devices, per_device(): lax.psum(partial_sum.astype(jnp.bfloat16), 'tensor').astype(jnp.float32)  29.8 us
    scatter x1, local copies, waits for them, and re-layouts, per_device(): jnp.full((owners, slots), -1, jnp.int32).at[expert_ids, slot]  22 us
    all_to_all x1, starting transfers between devices, per_device(): lax.all_to_all(owned, ('dp', 'expert'), split_axis=0, concat_axis=0, tile...  14.3 us
    reduce_scatter x1, waiting for transfers between devices, per_device(): lax.psum_scatter(expert_part.astype(jnp.bfloat16), 'tensor', scatter_dime...  11.5 us
    gather x2, local copies, waits for them, and re-layouts, per_device(): normed[jnp.maximum(owner_rows, 0)]  10.5 us
  transfers between devices with their start and end apart: 4, of which 4 were waited for; matrix products, arithmetic and copies ran while one was open for 11% of the time, Pallas kernels for 0%

commit v1 on v0

--- a/solution.py
+++ b/solution.py
@@ -63,7 +63,9 @@
     attended = attend_local(queries, fresh_keys, fresh_values, resident_keys, resident_values)
     partial_sum = jnp.dot(
         attended,
-        lax.all_gather(out_weight, "dp", axis=1, tiled=True),
+        jnp.concatenate(
+            lax.all_to_all(jnp.stack([out_weight] * lax.axis_size("dp")), "dp", 0, 0), axis=1
+        ),
         preferred_element_type=jnp.float32,
     )
     tokens_here = residual.shape[0]

time: 380 us -> 400 us (1.053)
  local copies, waits for them, and re-layouts: 60 us -> 70.2 us
  starting transfers between devices: 14.6 us -> 20 us
    all_to_all x0 -> x1, waiting for transfers between devices: none -> 53.9 us  [per_device(): lax.all_to_all(jnp.stack([out_weight] * lax.axis_size('dp')), 'dp', 0, 0)]
    all_gather x1 -> x0, waiting for transfers between devices: 50.1 us -> none  [per_device(): lax.all_gather(out_weight, 'dp', axis=1, tiled=True)]
    another operation x0 -> x1, local copies, waits for them, and re-layouts: none -> 5.89 us  [per_device(): jnp.stack([out_weight] * lax.axis_size('dp'))]
    all_to_all x0 -> x1, starting transfers between devices: none -> 5.65 us  [per_device(): lax.all_to_all(jnp.stack([out_weight] * lax.axis_size('dp')), 'dp', 0, 0)]
    unnamed x27 -> x28, local copies, waits for them, and re-layouts: 3.26 us -> 7.36 us
  transfers between devices with their start and end apart: 4 -> 4, of which waited for: 4 -> 4; matrix products, arithmetic and copies ran while one was open for 11% -> 10% of each run, Pallas kernels for 0% -> 0%
where the time goes in v1:
time: 400 us; the launch traced here: 399 us
  waiting for transfers between devices  147 us (37%)
  blocking collectives  111 us (28%)
  local copies, waits for them, and re-layouts  70.2 us (18%)
  matrix products  26 us (6%)
  starting transfers between devices  20 us (5%)
  between operations  13.7 us (3%)
  other arithmetic  10.8 us (3%)
    all_to_all x1, blocking collectives, per_device(): lax.all_to_all(outgoing, ('dp', 'expert'), split_axis=0, concat_axis=0, t...  111 us
    all_to_all x1, waiting for transfers between devices, per_device(): lax.all_to_all(jnp.stack([out_weight] * lax.axis_size('dp')), 'dp', 0, 0)  53.9 us
    all_to_all x1, waiting for transfers between devices, per_device(): lax.all_to_all(owned, ('dp', 'expert'), split_axis=0, concat_axis=0, tile...  52.1 us
    psum x1, waiting for transfers between devices, per_device(): lax.psum(partial_sum.astype(jnp.bfloat16), 'tensor').astype(jnp.float32)  29.7 us
    scatter x1, local copies, waits for them, and re-layouts, per_device(): jnp.full((owners, slots), -1, jnp.int32).at[expert_ids, slot]  22.2 us
    all_to_all x1, starting transfers between devices, per_device(): lax.all_to_all(owned, ('dp', 'expert'), split_axis=0, concat_axis=0, tile...  14.3 us
    reduce_scatter x1, waiting for transfers between devices, per_device(): lax.psum_scatter(expert_part.astype(jnp.bfloat16), 'tensor', scatter_dime...  11.5 us
    gather x2, local copies, waits for them, and re-layouts, per_device(): normed[jnp.maximum(owner_rows, 0)]  10.5 us
  transfers between devices with their start and end apart: 4, of which 4 were waited for; matrix products, arithmetic and copies ran while one was open for 10% of the time, Pallas kernels for 0%

profile of v1, /device:TPU:32, one launch (start us, length us, event | category | flops | bytes accessed | tf_op | source)
XLA Modules:
  0.0 399.2 jit_solution(9512298692952138060)
XLA Ops:
  6.5 0.0 copy-start
  6.5 4.1 %copy.82 = bf16[2048,512]{0,1:T(8,128)(2,1)} copy(bf16[2048,512]{1,0:T(8,128)(2,1)} %param.18) | data formatting | bytes 4194304 | tf_op args[5]
  10.6 5.9 %stack.2 = bf16[4,2048,512]{1,2,0:T(8,128)(2,1)} broadcast(bf16[2048,512]{0,1:T(8,128)(2,1)} %copy.82), dimensions={1,2} | broadcast | bytes 10485760 | tf_op jit(solution)/shard_map/stack | solution.py:67
  16.5 5.7 %all-to-all-start = ((bf16[4,2048,512]{1,2,0:T(8,128)(2,1)}), bf16[4,2048,512]{1,2,0:T(8,128)(2,1)}, u32[]{:S(2)}, u32[]{:S(2)}) async-start(bf16[4,2048,512]{1,2,0:T(8,128)(2,1)} %stack.2), calls=%async_computation | async-start | bytes 16777216 | tf_op jit(solution)/shard_map/all_to_all | solution.py:67
  22.2 0.0 copy-start.4
  22.2 0.0 all-reduce.2.cloned.1.call-start
  22.2 1.5 copy.77
  23.8 1.3 copy.78
  25.1 0.0 copy-done.4
  25.1 0.0 copy-start.5
  25.2 0.0 copy-start.6
  25.2 1.5 copy.74
  26.7 1.3 copy.75
  28.0 0.0 copy-done.5
  28.0 0.0 copy-done.6
  28.1 0.1 fusion.26
  28.2 0.0 copy-start.2
  28.2 4.6 %fusion.46 = f32[2,8,64]{2,1,0:T(8,128)S(1)} fusion(pred[64,2112]{1,0:T(8,128)(4,1)S(1)} %fusion.26, bf16[64,2,128]{2,0,1:T(8,128)(2,1)S(1)} %get-tuple-element.9, bf16[2048,2,128]{2,0,1:T(8,128)(2,1)} %copy.78, bf16[64,2,8,128]{3,2,1,0:T(8,128)(2,1)S(1)} %bitcast.100), kind=kOutput, calls=%fused_computation.69 | convolution fusion | flops 564463680 | bytes 1482752 | tf_op jit(solution)/shard_map/sub | solution.py:30
  32.8 0.0 copy-done.2
  32.8 4.9 %fusion.19 = bf16[64,2,8,128]{3,0,2,1:T(8,128)(2,1)S(1)} fusion(f32[2,8,64]{2,1,0:T(8,128)S(1)} %fusion.46, bf16[64,2,128]{2,0,1:T(8,128)(2,1)S(1)} %get-tuple-element.10, bf16[2048,2,128]{2,0,1:T(8,128)(2,1)} %copy.75, pred[64,2112]{1,0:T(8,128)(4,1)S(1)} %fusion.26, bf16[64,2,128]{2,0,1:T(8,128)(2,1)S(1)} %get-tuple-element.9, ...), kind=kOutput, calls=%fused_computation.25 | convolution fusion | flops 1122569216 | bytes 2826240 | tf_op jit(solution)/shard_map/jgts,sjd->tjgd/dot_general | solution.py:32
  37.7 0.2 copy.81
  37.9 0.0 copy-done.7
  37.9 0.1 copy.84
  38.0 0.1 convert_reduce_fusion
  38.2 0.1 reduce_window_sum.11
  38.3 1.2 select_reduce_fusion
  39.5 0.1 copy.85
  39.6 0.1 copy.86
  39.7 0.1 reshape.90
  39.8 0.1 reshape.92
  39.9 22.2 %scatter_fusion = s32[128,6]{0,1:T(8,128)S(1)} fusion(s32[128,6]{0,1:T(8,128)S(1)} %broadcast_in_dim.26, s32[512]{0:T(512)S(1)} %reshape.90, s32[512]{0:T(512)S(1)} %reshape.92), kind=kCustom, calls=%fused_computation.2 | custom fusion | bytes 10240 | tf_op jit(solution)/shard_map/scatter | solution.py:90
  62.1 0.1 copy.88
  62.2 0.1 reshape.78
  62.3 53.9 %all-to-all-done = bf16[4,2048,512]{1,2,0:T(8,128)(2,1)} async-done(((bf16[4,2048,512]{1,2,0:T(8,128)(2,1)}), bf16[4,2048,512]{1,2,0:T(8,128)(2,1)}, u32[]{:S(2)}, u32[]{:S(2)}) %all-to-all-start) | async-done | bytes 8388640 | tf_op jit(solution)/shard_map/all_to_all | solution.py:67
  116.3 6.8 %convolution_convert_fusion.1 = bf16[64,2048]{1,0:T(8,128)(2,1)} fusion(bf16[2048,2048]{0,1:T(8,128)(2,1)} %bitcast.9, bf16[8,8,16,128]{3,2,1,0:T(8,128)(2,1)S(1)} %bitcast.98), kind=kOutput, calls=%fused_computation.14 | convolution fusion | flops 537001984 | bytes 8912896 | tf_op jit(solution)/shard_map/dot_general | solution.py:64
  123.1 0.0 all-reduce.2.cloned.1.call-update
  123.1 0.0 reduce-scatter.2.cloned.1.call-start
  123.1 0.1 copy.87
  123.3 29.7 %all-reduce.2.cloned.1.call-done = bf16[64,2048]{1,0:T(8,128)(2,1)} async-done(((bf16[64,2048]{1,0:T(8,128)(2,1)}), bf16[64,2048]{1,0:T(8,128)(2,1)}) %all-reduce.2.cloned.1.call-update) | async-done | bytes 262160 | tf_op jit(solution)/shard_map/psum | solution.py:75
  153.0 0.0 copy-done.3
  153.0 1.9 convert_add_fusion
  155.0 0.0 copy-done.8
  155.0 1.1 multiply_convert_fusion
  156.1 4.3 %gather_fusion = bf16[768,2048]{1,0:T(8,128)(2,1)} fusion(bf16[64,2048]{1,0:T(8,128)(2,1)S(1)} %multiply_convert_fusion, s32[1024]{0:T(1024)S(1)} %pad_clamp_fusion), kind=kCustom, calls=%fused_computation | custom fusion | bytes 6294528 | tf_op jit(solution)/shard_map/gather | solution.py:93
  160.3 6.3 %reshape.77 = bf16[128,6,2048]{2,1,0:T(8,128)(2,1)} reshape(bf16[768,2048]{1,0:T(8,128)(2,1)} %gather_fusion) | data formatting | bytes 6291456 | tf_op jit(solution)/shard_map/gather | solution.py:93
  166.6 2.6 broadcast_select_fusion
  169.2 111.2 %all_to_all.15 = bf16[128,6,2048]{2,1,0:T(8,128)(2,1)} all-to-all(bf16[128,6,2048]{2,1,0:T(8,128)(2,1)S(1)} %broadcast_select_fusion), channel_id=1, replica_groups=mesh['dp'=4,'expert'=32,'tensor'=2] {'dp','expert'}, dimensions={0} | all-to-all | bytes 6291456 | tf_op jit(solution)/shard_map/all_to_all | solution.py:96
  280.5 6.3 %reshape.75 = bf16[768,2048]{1,0:T(8,128)(2,1)} reshape(bf16[128,6,2048]{2,1,0:T(8,128)(2,1)} %all_to_all.15) | data formatting | bytes 6291456 | tf_op jit(solution)/shard_map/reshape | solution.py:40
  286.8 4.3 %fusion.10 = f32[768,384]{1,0:T(8,128)S(1)} fusion(bf16[768,2048]{1,0:T(8,128)(2,1)} %reshape.75, bf16[1,2048,384]{2,1,0:T(8,128)(2,1)} %param.23), kind=kOutput, calls=%fused_computation.20 | convolution fusion | flops 1207959552 | bytes 5898240 | tf_op jit(solution)/shard_map/dot_general | solution.py:41
  291.1 1.8 fusion.15
  293.0 0.2 dot_general.25
  293.2 3.5 convolution_convert_fusion
  296.7 0.0 reduce-scatter.2.cloned.1.call-update
  296.7 11.5 %reduce-scatter.2.cloned.1.call-done = bf16[128,6,1024]{2,0,1:T(8,128)(2,1)} async-done(((bf16[128,6,2048]{2,0,1:T(8,128)(2,1)}), bf16[128,6,1024]{2,0,1:T(8,128)(2,1)}) %reduce-scatter.2.cloned.1.call-update) | async-done | bytes 1572880 | tf_op jit(solution)/shard_map/reduce_scatter | solution.py:101
  308.2 3.6 copy.90
  311.8 14.3 %all-to-all-start.2 = ((bf16[128,6,1024]{2,1,0:T(8,128)(2,1)}), bf16[128,6,1024]{2,1,0:T(8,128)(2,1)}, u32[]{:S(2)}, u32[]{:S(2)}) async-start(bf16[128,6,1024]{2,1,0:T(8,128)(2,1)} %copy.90), calls=%async_computation.3 | async-start | bytes 4194304 | tf_op jit(solution)/shard_map/all_to_all | solution.py:104
  326.1 0.1 copy.91
  326.2 0.1 reshape.84
  326.3 0.1 copy.83
  326.4 52.1 %all-to-all-done.2 = bf16[128,6,1024]{2,1,0:T(8,128)(2,1)} async-done(((bf16[128,6,1024]{2,1,0:T(8,128)(2,1)}), bf16[128,6,1024]{2,1,0:T(8,128)(2,1)}, u32[]{:S(2)}, u32[]{:S(2)}) %all-to-all-start.2) | async-done | bytes 1572896 | tf_op jit(solution)/shard_map/all_to_all | solution.py:104
  378.4 2.5 copy.92
  380.9 7.9 %gather_fusion.1 = bf16[512,1024]{1,0:T(8,128)(2,1)} fusion(bf16[128,6,1024]{2,0,1:T(8,128)(2,1)S(1)} %copy.92, s32[512]{0:T(512)S(1)} %reshape.84), kind=kCustom, calls=%fused_computation.1 | custom fusion | bytes 2101248 | tf_op jit(solution)/shard_map/gather | solution.py:105
  388.8 1.9 fusion.6
  390.7 1.6 add_convert_fusion
  (22 shorter events, 0.1 us)
Async XLA Ops:
  6.5 286.7 %copy-start = (bf16[1,384,2048]{2,1,0:T(8,128)(2,1)S(1)}, bf16[1,384,2048]{2,1,0:T(8,128)(2,1)}, u32[]{:S(2)}) copy-start(bf16[1,384,2048]{2,1,0:T(8,128)(2,1)} %param.25) | copy-start | bytes 4718596
  16.5 99.7 %all-to-all-start = ((bf16[4,2048,512]{1,2,0:T(8,128)(2,1)}), bf16[4,2048,512]{1,2,0:T(8,128)(2,1)}, u32[]{:S(2)}, u32[]{:S(2)}) async-start(bf16[4,2048,512]{1,2,0:T(8,128)(2,1)} %stack.2), calls=%async_computation | async-start | bytes 16777216 | tf_op jit(solution)/shard_map/all_to_all | solution.py:67
  22.2 2.9 copy-start.4
  22.2 130.8 %all-reduce.2.cloned.1.call-start = ((), (), s32[]{:S(2)}) async-start(), calls=%async_computation.4 | async-start | bytes 524288 | tf_op jit(solution)/shard_map/psum | solution.py:75
  25.1 2.9 copy-start.5
  25.2 2.9 copy-start.6
  28.2 4.7 %copy-start.2 = (bf16[2048,2,128]{2,0,1:T(8,128)(2,1)S(1)}, bf16[2048,2,128]{2,0,1:T(8,128)(2,1)}, u32[]{:S(2)}) copy-start(bf16[2048,2,128]{2,0,1:T(8,128)(2,1)} %copy.78) | copy-start | bytes 3145732
  32.8 5.1 %copy-start.7 = (s32[64,8]{0,1:T(8,128)S(1)}, s32[64,8]{0,1:T(8,128)}, u32[]{:S(2)}) copy-start(s32[64,8]{0,1:T(8,128)} %param.21) | copy-start | bytes 6148
  116.3 36.8 %copy-start.3 = (bf16[64,2048]{1,0:T(8,128)(2,1)S(1)}, bf16[64,2048]{1,0:T(8,128)(2,1)}, u32[]{:S(2)}) copy-start(bf16[64,2048]{1,0:T(8,128)(2,1)} %param.19) | copy-start | bytes 786436
  116.3 38.7 %copy-start.8 = (f32[2048]{0:T(1024)S(1)}, f32[2048]{0:T(1024)}, u32[]{:S(2)}) copy-start(f32[2048]{0:T(1024)} %param.20) | copy-start | bytes 24580
  123.1 185.1 %reduce-scatter.2.cloned.1.call-start = ((), (), s32[]{:S(2)}) async-start(), calls=%async_computation.5 | async-start | bytes 4718592 | tf_op jit(solution)/shard_map/reduce_scatter | solution.py:101
  286.8 4.3 %copy-start.1 = (bf16[768,2048]{1,0:T(8,128)(2,1)S(1)}, bf16[768,2048]{1,0:T(8,128)(2,1)}, u32[]{:S(2)}) copy-start(bf16[768,2048]{1,0:T(8,128)(2,1)} %reshape.75) | copy-start | bytes 9437188
  286.8 4.3 %copy-start.10 = (bf16[1,2048,384]{2,1,0:T(8,128)(2,1)S(1)}, bf16[1,2048,384]{2,1,0:T(8,128)(2,1)}, u32[]{:S(2)}) copy-start(bf16[1,2048,384]{2,1,0:T(8,128)(2,1)} %param.24) | copy-start | bytes 4718596
  311.8 14.5 %copy-start.9 = (f32[64,8]{0,1:T(8,128)S(1)}, f32[64,8]{0,1:T(8,128)}, u32[]{:S(2)}) copy-start(f32[64,8]{0,1:T(8,128)} %param.22) | copy-start | bytes 6148
  311.8 66.6 %all-to-all-start.2 = ((bf16[128,6,1024]{2,1,0:T(8,128)(2,1)}), bf16[128,6,1024]{2,1,0:T(8,128)(2,1)}, u32[]{:S(2)}, u32[]{:S(2)}) async-start(bf16[128,6,1024]{2,1,0:T(8,128)(2,1)} %copy.90), calls=%async_computation.3 | async-start | bytes 4194304 | tf_op jit(solution)/shard_map/all_to_all | solution.py:104
Sparse Core Ops, SparseCore 0:
  123.2 29.7 all-reduce.1
  296.8 11.3 reduce-scatter.1
